TPU v7x, 256 devices: a whole 4x4x8 slice. The times are simulated.
256 devices in a mesh: ctx: 32 (over y, x, core), fsdp: 4 (over z_hi), tp: 2 (over z_lo).
Axes of the slice: x: 4, y: 4, z: 8 (z_hi: 4, z_lo: 2; z = z_hi * 2 + z_lo), core: 2. Of those that a mesh axis runs over, the one named last changes fastest.
Arguments:
- query_gate: bfloat16 [4, 4096, 8192], P('fsdp', 'ctx', 'tp'), may hold values from -6 to 6
- key_proj: bfloat16 [4, 4096, 8192], P('fsdp', 'ctx', 'tp'), may hold values from -6 to 6
- value_proj: bfloat16 [4, 4096, 8192], P('fsdp', 'ctx', 'tp'), may hold values from -6 to 6
- grad_out: bfloat16 [4, 4096, 8192], P('fsdp', 'ctx', 'tp'), may hold values from -6 to 6
- filters: float32 [128, 8192], P('fsdp', 'tp'), may hold values from -0.5 to 0.5
- doc_bounds: int32 [4, 49], P('fsdp'), may hold values from 0 to 4032, as said below
- continues: int32 [4, 32], P('fsdp', 'ctx'), may hold values from 0 to 1, as said below
Outputs:
- grad_query: bfloat16 [4, 4096, 8192], P('fsdp', 'ctx', 'tp')
- grad_key: bfloat16 [4, 4096, 8192], P('fsdp', 'ctx', 'tp')
- grad_value: bfloat16 [4, 4096, 8192], P('fsdp', 'ctx', 'tp')
- grad_filter: float32 [128, 8192], P('fsdp', 'tp')
Inputs may be any that keep to these rules, and one draw needn't show every extreme that they name: Each row of doc_bounds increases strictly and begins with 0. continues[w, d] is 0 for d = 0 and wherever a document of window w begins at token d * 128; at other shard edges it may be 0 or 1 (the sequence is cut there or not).
All inputs are finite; a program needn't handle non-finite values.
Results may differ from a plain program's by a relative error of at most 0.0065.
Values may be sent and summed in bfloat16 or wider, within the bound.
A program may use at most 64 MiB of HBM per device.

v0:
```python
import math
import jax
import jax.numpy as jnp
from jax import lax
from jax.sharding import PartitionSpec as P

tap_group = 16


def from_behind(array, axis, by):
    count = lax.axis_size(axis)
    pairs = [(i, i + by) for i in range(count) if 0 <= i + by < count]
    return lax.ppermute(array, axis, pairs)


def doc_starts(bound_row, positions):
    below = bound_row[None, :] <= positions[:, None]
    return jnp.max(jnp.where(below, bound_row[None, :], 0), axis=1)


def shards(query_gate, key_proj, value_proj, grad_out, filters, doc_bounds, continues):
    weights = lax.all_gather(filters, "fsdp", axis=0, tiled=True)
    filter_len = weights.shape[0]
    length = query_gate.shape[1]
    shard_index = lax.axis_index("ctx")
    first_token = shard_index * length
    positions = first_token + jnp.arange(length, dtype=jnp.int32)
    bound_row = doc_bounds[0]
    own_flag = continues[0, 0]
    plain_starts = doc_starts(bound_row, positions)
    own_starts = jnp.where(own_flag == 1, plain_starts, jnp.maximum(plain_starts, first_token))
    later_positions = first_token + length + jnp.arange(filter_len, dtype=jnp.int32)
    reach_starts = jnp.concatenate([own_starts, doc_starts(bound_row, later_positions)])
    query_local = query_gate[0]
    key_local = key_proj[0]
    value_local = value_proj[0]
    grad_local = grad_out[0]
    channels = query_local.shape[1]
    mixed_input = (key_local.astype(jnp.float32) * value_local.astype(jnp.float32)).astype(
        jnp.bfloat16
    )
    rows_before = from_behind(mixed_input, "ctx", 1)
    mixed_ext = jnp.concatenate([rows_before, mixed_input], axis=0)
    grad_conv = (grad_local.astype(jnp.float32) * query_local.astype(jnp.float32)).astype(
        jnp.bfloat16
    )
    send_rows = jnp.where(own_flag == 1, grad_conv, jnp.zeros_like(grad_conv))
    rows_after = from_behind(send_rows, "ctx", -1)
    grad_ext = jnp.concatenate([grad_conv, rows_after], axis=0)
    grad_wide = grad_conv.astype(jnp.float32)

    def tap_block(group_index, state_tuple):
        conv_out, grad_back, filt_grad = state_tuple
        for offset in range(tap_group):
            tap_index = group_index * tap_group + offset
            weight_row = lax.dynamic_slice_in_dim(weights, tap_index, 1, 0)
            earlier = lax.dynamic_slice_in_dim(mixed_ext, filter_len - tap_index, length, 0).astype(
                jnp.float32
            )
            inside = (positions - tap_index >= own_starts)[:, None]
            conv_out = conv_out + jnp.where(inside, earlier * weight_row, 0.0)
            tap_term = jnp.sum(jnp.where(inside, grad_wide * earlier, 0.0), axis=0)
            filt_grad = lax.dynamic_update_slice_in_dim(filt_grad, tap_term[None, :], tap_index, 0)
            ahead_rows = lax.dynamic_slice_in_dim(grad_ext, tap_index, length, 0).astype(
                jnp.float32
            )
            reaching = (positions >= lax.dynamic_slice_in_dim(reach_starts, tap_index, length, 0))[
                :, None
            ]
            grad_back = grad_back + jnp.where(reaching, ahead_rows * weight_row, 0.0)
        return (conv_out, grad_back, filt_grad)

    start_state = (
        jnp.zeros((length, channels), jnp.float32),
        jnp.zeros((length, channels), jnp.float32),
        jnp.zeros((filter_len, channels), jnp.float32),
    )
    conv_out, grad_back, filt_grad = lax.fori_loop(
        jnp.int32(0), jnp.int32(filter_len // tap_group), tap_block, start_state
    )
    grad_query = (grad_local.astype(jnp.float32) * conv_out).astype(jnp.bfloat16)
    grad_key = (grad_back * value_local.astype(jnp.float32)).astype(jnp.bfloat16)
    grad_value = (grad_back * key_local.astype(jnp.float32)).astype(jnp.bfloat16)
    norm_scale = 1.0 / math.sqrt(lax.axis_size("fsdp") * lax.axis_size("ctx") * length)
    filt_grad = filt_grad * norm_scale
    summed_all = lax.psum(filt_grad, "ctx")
    share_out = lax.psum_scatter(summed_all, "fsdp", scatter_dimension=0, tiled=True)
    return (grad_query[None], grad_key[None], grad_value[None], share_out)


def solution(mesh):
    in_specs = (
        P("fsdp", "ctx", "tp"),
        P("fsdp", "ctx", "tp"),
        P("fsdp", "ctx", "tp"),
        P("fsdp", "ctx", "tp"),
        P("fsdp", "tp"),
        P("fsdp", None),
        P("fsdp", "ctx"),
    )
    out_specs = (
        P("fsdp", "ctx", "tp"),
        P("fsdp", "ctx", "tp"),
        P("fsdp", "ctx", "tp"),
        P("fsdp", "tp"),
    )
    return jax.shard_map(shards, mesh=mesh, in_specs=in_specs, out_specs=out_specs, check_vma=False)
```

profile of v0, /device:TPU:1, one launch (start us, length us, event | category | flops | bytes accessed | tf_op | source)
XLA Modules:
  0.0 783.8 jit_solution(15440662783563626389)
XLA Ops:
  20.8 5.3 collective-permute-done
  28.0 6.5 collective-permute-done.1
  37.2 25.2 %all-gather.2.cloned.1.call-done = f32[128,4096]{1,0:T(8,128)} async-done(((f32[32,4096]{1,0:T(8,128)}), f32[128,4096]{1,0:T(8,128)}) %all-gather.2.cloned.1.call-update) | async-done | bytes 2097168 | tf_op jit(solution)/shard_map/all_gather | solution.py:22
  63.9 540.4 %while.18 = (s32[]{:T(128)}, f32[128,4096]{1,0:T(8,128)}, f32[128,4096]{1,0:T(8,128)}, f32[128,4096]{1,0:T(8,128)}, s32[128]{0:T(128)S(1)}, /*index=5*/bf16[256,...) while((s32[]{:T(128)}, f32[128,4096]{1,0:T(8,128)}, ...), condition=%wide.region_19.20_spmd.clone, body=%wide.region_2.19_spmd.clone.sunk | while | flops 101652864 | bytes 89937200 | solution.py:78
  64.1 6.7 fusion.150
  70.8 5.3 fusion.149
  104.1 15.4 %fusion.148 = f32[128,4096]{1,0:T(8,128)} fusion(f32[128,4096]{1,0:T(8,128)} %get-tuple-element.669, bf16[256,4096]{1,0:T(8,128)(2,1)} %get-tuple-element.736, s32[]{:T(128)S(6)} %select_n.1126, s32[]{:T(128)S(6)} %select_n.1127, s32[]{:T(128)S(6)} %select_n.1128, s32[]{:T(128)S(6)} %select_n.1129, s32[]{:T(128)S(6)} %select_n.1130, ...), kind=kLoop, calls=%fused_computation.112.clone.1 | loop fusion | flops 34078720 | bytes 21235776 | tf_op jit(solution)/shard_map/while/body/add | solution.py:70
  119.5 10.1 %fusion.146 = f32[128,4096]{1,0:T(8,128)S(1)} fusion(f32[128,4096]{1,0:T(8,128)S(1)} %copy-done.2, f32[4096]{0:T(1024)S(1)} %bitcast.124, f32[4096]{0:T(1024)S(1)} %bitcast.126, f32[4096]{0:T(1024)S(1)} %bitcast.128, f32[4096]{0:T(1024)S(1)} %bitcast.130, f32[4096]{0:T(1024)S(1)} %bitcast.132, f32[4096]{0:T(1024)S(1)} %bitcast.134, ...), kind=kLoop, calls=%fused_computation.49.clone.1 | loop fusion | flops 34078720 | bytes 21235776 | tf_op jit(solution)/shard_map/while/body/add | solution.py:61
  131.2 6.7 fusion.150
  137.9 5.3 fusion.149
  171.3 15.7 %fusion.148 = f32[128,4096]{1,0:T(8,128)} fusion(f32[128,4096]{1,0:T(8,128)} %get-tuple-element.669, bf16[256,4096]{1,0:T(8,128)(2,1)} %get-tuple-element.736, s32[]{:T(128)S(6)} %select_n.1126, s32[]{:T(128)S(6)} %select_n.1127, s32[]{:T(128)S(6)} %select_n.1128, s32[]{:T(128)S(6)} %select_n.1129, s32[]{:T(128)S(6)} %select_n.1130, ...), kind=kLoop, calls=%fused_computation.112.clone.1 | loop fusion | flops 34078720 | bytes 21235776 | tf_op jit(solution)/shard_map/while/body/add | solution.py:70
  187.1 10.1 %fusion.146 = f32[128,4096]{1,0:T(8,128)S(1)} fusion(f32[128,4096]{1,0:T(8,128)S(1)} %copy-done.2, f32[4096]{0:T(1024)S(1)} %bitcast.124, f32[4096]{0:T(1024)S(1)} %bitcast.126, f32[4096]{0:T(1024)S(1)} %bitcast.128, f32[4096]{0:T(1024)S(1)} %bitcast.130, f32[4096]{0:T(1024)S(1)} %bitcast.132, f32[4096]{0:T(1024)S(1)} %bitcast.134, ...), kind=kLoop, calls=%fused_computation.49.clone.1 | loop fusion | flops 34078720 | bytes 21235776 | tf_op jit(solution)/shard_map/while/body/add | solution.py:61
  198.7 6.7 fusion.150
  238.9 15.9 %fusion.148 = f32[128,4096]{1,0:T(8,128)} fusion(f32[128,4096]{1,0:T(8,128)} %get-tuple-element.669, bf16[256,4096]{1,0:T(8,128)(2,1)} %get-tuple-element.736, s32[]{:T(128)S(6)} %select_n.1126, s32[]{:T(128)S(6)} %select_n.1127, s32[]{:T(128)S(6)} %select_n.1128, s32[]{:T(128)S(6)} %select_n.1129, s32[]{:T(128)S(6)} %select_n.1130, ...), kind=kLoop, calls=%fused_computation.112.clone.1 | loop fusion | flops 34078720 | bytes 21235776 | tf_op jit(solution)/shard_map/while/body/add | solution.py:70
  254.9 10.1 %fusion.146 = f32[128,4096]{1,0:T(8,128)S(1)} fusion(f32[128,4096]{1,0:T(8,128)S(1)} %copy-done.2, f32[4096]{0:T(1024)S(1)} %bitcast.124, f32[4096]{0:T(1024)S(1)} %bitcast.126, f32[4096]{0:T(1024)S(1)} %bitcast.128, f32[4096]{0:T(1024)S(1)} %bitcast.130, f32[4096]{0:T(1024)S(1)} %bitcast.132, f32[4096]{0:T(1024)S(1)} %bitcast.134, ...), kind=kLoop, calls=%fused_computation.49.clone.1 | loop fusion | flops 34078720 | bytes 21235776 | tf_op jit(solution)/shard_map/while/body/add | solution.py:61
  266.5 6.7 fusion.150
  306.4 16.0 %fusion.148 = f32[128,4096]{1,0:T(8,128)} fusion(f32[128,4096]{1,0:T(8,128)} %get-tuple-element.669, bf16[256,4096]{1,0:T(8,128)(2,1)} %get-tuple-element.736, s32[]{:T(128)S(6)} %select_n.1126, s32[]{:T(128)S(6)} %select_n.1127, s32[]{:T(128)S(6)} %select_n.1128, s32[]{:T(128)S(6)} %select_n.1129, s32[]{:T(128)S(6)} %select_n.1130, ...), kind=kLoop, calls=%fused_computation.112.clone.1 | loop fusion | flops 34078720 | bytes 21235776 | tf_op jit(solution)/shard_map/while/body/add | solution.py:70
  322.5 10.1 %fusion.146 = f32[128,4096]{1,0:T(8,128)S(1)} fusion(f32[128,4096]{1,0:T(8,128)S(1)} %copy-done.2, f32[4096]{0:T(1024)S(1)} %bitcast.124, f32[4096]{0:T(1024)S(1)} %bitcast.126, f32[4096]{0:T(1024)S(1)} %bitcast.128, f32[4096]{0:T(1024)S(1)} %bitcast.130, f32[4096]{0:T(1024)S(1)} %bitcast.132, f32[4096]{0:T(1024)S(1)} %bitcast.134, ...), kind=kLoop, calls=%fused_computation.49.clone.1 | loop fusion | flops 34078720 | bytes 21235776 | tf_op jit(solution)/shard_map/while/body/add | solution.py:61
  334.1 6.7 fusion.150
  374.2 15.8 %fusion.148 = f32[128,4096]{1,0:T(8,128)} fusion(f32[128,4096]{1,0:T(8,128)} %get-tuple-element.669, bf16[256,4096]{1,0:T(8,128)(2,1)} %get-tuple-element.736, s32[]{:T(128)S(6)} %select_n.1126, s32[]{:T(128)S(6)} %select_n.1127, s32[]{:T(128)S(6)} %select_n.1128, s32[]{:T(128)S(6)} %select_n.1129, s32[]{:T(128)S(6)} %select_n.1130, ...), kind=kLoop, calls=%fused_computation.112.clone.1 | loop fusion | flops 34078720 | bytes 21235776 | tf_op jit(solution)/shard_map/while/body/add | solution.py:70
  390.0 10.1 %fusion.146 = f32[128,4096]{1,0:T(8,128)S(1)} fusion(f32[128,4096]{1,0:T(8,128)S(1)} %copy-done.2, f32[4096]{0:T(1024)S(1)} %bitcast.124, f32[4096]{0:T(1024)S(1)} %bitcast.126, f32[4096]{0:T(1024)S(1)} %bitcast.128, f32[4096]{0:T(1024)S(1)} %bitcast.130, f32[4096]{0:T(1024)S(1)} %bitcast.132, f32[4096]{0:T(1024)S(1)} %bitcast.134, ...), kind=kLoop, calls=%fused_computation.49.clone.1 | loop fusion | flops 34078720 | bytes 21235776 | tf_op jit(solution)/shard_map/while/body/add | solution.py:61
  401.6 6.7 fusion.150
  441.6 15.6 %fusion.148 = f32[128,4096]{1,0:T(8,128)} fusion(f32[128,4096]{1,0:T(8,128)} %get-tuple-element.669, bf16[256,4096]{1,0:T(8,128)(2,1)} %get-tuple-element.736, s32[]{:T(128)S(6)} %select_n.1126, s32[]{:T(128)S(6)} %select_n.1127, s32[]{:T(128)S(6)} %select_n.1128, s32[]{:T(128)S(6)} %select_n.1129, s32[]{:T(128)S(6)} %select_n.1130, ...), kind=kLoop, calls=%fused_computation.112.clone.1 | loop fusion | flops 34078720 | bytes 21235776 | tf_op jit(solution)/shard_map/while/body/add | solution.py:70
  457.3 10.1 %fusion.146 = f32[128,4096]{1,0:T(8,128)S(1)} fusion(f32[128,4096]{1,0:T(8,128)S(1)} %copy-done.2, f32[4096]{0:T(1024)S(1)} %bitcast.124, f32[4096]{0:T(1024)S(1)} %bitcast.126, f32[4096]{0:T(1024)S(1)} %bitcast.128, f32[4096]{0:T(1024)S(1)} %bitcast.130, f32[4096]{0:T(1024)S(1)} %bitcast.132, f32[4096]{0:T(1024)S(1)} %bitcast.134, ...), kind=kLoop, calls=%fused_computation.49.clone.1 | loop fusion | flops 34078720 | bytes 21235776 | tf_op jit(solution)/shard_map/while/body/add | solution.py:61
  468.9 6.7 fusion.150
  508.9 16.1 %fusion.148 = f32[128,4096]{1,0:T(8,128)} fusion(f32[128,4096]{1,0:T(8,128)} %get-tuple-element.669, bf16[256,4096]{1,0:T(8,128)(2,1)} %get-tuple-element.736, s32[]{:T(128)S(6)} %select_n.1126, s32[]{:T(128)S(6)} %select_n.1127, s32[]{:T(128)S(6)} %select_n.1128, s32[]{:T(128)S(6)} %select_n.1129, s32[]{:T(128)S(6)} %select_n.1130, ...), kind=kLoop, calls=%fused_computation.112.clone.1 | loop fusion | flops 34078720 | bytes 21235776 | tf_op jit(solution)/shard_map/while/body/add | solution.py:70
  525.0 10.1 %fusion.146 = f32[128,4096]{1,0:T(8,128)S(1)} fusion(f32[128,4096]{1,0:T(8,128)S(1)} %copy-done.2, f32[4096]{0:T(1024)S(1)} %bitcast.124, f32[4096]{0:T(1024)S(1)} %bitcast.126, f32[4096]{0:T(1024)S(1)} %bitcast.128, f32[4096]{0:T(1024)S(1)} %bitcast.130, f32[4096]{0:T(1024)S(1)} %bitcast.132, f32[4096]{0:T(1024)S(1)} %bitcast.134, ...), kind=kLoop, calls=%fused_computation.49.clone.1 | loop fusion | flops 34078720 | bytes 21235776 | tf_op jit(solution)/shard_map/while/body/add | solution.py:61
  536.6 6.7 fusion.150
  576.9 16.1 %fusion.148 = f32[128,4096]{1,0:T(8,128)} fusion(f32[128,4096]{1,0:T(8,128)} %get-tuple-element.669, bf16[256,4096]{1,0:T(8,128)(2,1)} %get-tuple-element.736, s32[]{:T(128)S(6)} %select_n.1126, s32[]{:T(128)S(6)} %select_n.1127, s32[]{:T(128)S(6)} %select_n.1128, s32[]{:T(128)S(6)} %select_n.1129, s32[]{:T(128)S(6)} %select_n.1130, ...), kind=kLoop, calls=%fused_computation.112.clone.1 | loop fusion | flops 34078720 | bytes 21235776 | tf_op jit(solution)/shard_map/while/body/add | solution.py:70
  592.9 10.1 %fusion.146 = f32[128,4096]{1,0:T(8,128)S(1)} fusion(f32[128,4096]{1,0:T(8,128)S(1)} %copy-done.2, f32[4096]{0:T(1024)S(1)} %bitcast.124, f32[4096]{0:T(1024)S(1)} %bitcast.126, f32[4096]{0:T(1024)S(1)} %bitcast.128, f32[4096]{0:T(1024)S(1)} %bitcast.130, f32[4096]{0:T(1024)S(1)} %bitcast.132, f32[4096]{0:T(1024)S(1)} %bitcast.134, ...), kind=kLoop, calls=%fused_computation.49.clone.1 | loop fusion | flops 34078720 | bytes 21235776 | tf_op jit(solution)/shard_map/while/body/add | solution.py:61
  612.3 47.3 %reduce-scatter.2.cloned.1.call-done = f32[32,4096]{1,0:T(8,128)} async-done(((f32[128,4096]{1,0:T(8,128)}), f32[32,4096]{1,0:T(8,128)}) %reduce-scatter.2.cloned.1.call-update) | async-done | bytes 524304 | tf_op jit(solution)/shard_map/reduce_scatter | solution.py:87
  662.6 112.8 %all-reduce.2.cloned.1.call-done = f32[32,4096]{1,0:T(8,128)} async-done(((f32[32,4096]{1,0:T(8,128)}), f32[32,4096]{1,0:T(8,128)}) %all-reduce.2.cloned.1.call-update) | async-done | bytes 524304 | tf_op jit(solution)/shard_map/psum | solution.py:86
  (242 shorter events, 300.0 us)
Async XLA Ops:
  7.2 7.9 %copy-start.5 = (bf16[1,128,4096]{2,1,0:T(8,128)(2,1)S(1)}, bf16[1,128,4096]{2,1,0:T(8,128)(2,1)}, u32[]{:S(2)}) copy-start(bf16[1,128,4096]{2,1,0:T(8,128)(2,1)} %param.12) | copy-start | bytes 3145732
  7.2 55.2 %all-gather.2.cloned.1.call-start = ((), (), s32[]{:S(2)}) async-start(), calls=%async_computation.1 | async-start | bytes 2621440 | tf_op jit(solution)/shard_map/all_gather | solution.py:22
  7.9 651.6 %reduce-scatter.2.cloned.1.call-start = ((), (), s32[]{:S(2)}) async-start(), calls=%async_computation.2 | async-start | bytes 2621440 | tf_op jit(solution)/shard_map/reduce_scatter | solution.py:87
  8.0 7.1 copy-start.7
  9.8 6.8 copy-start.6
  9.9 16.2 %collective-permute-start = (bf16[128,4096]{1,0:T(8,128)(2,1)S(1)}, bf16[128,4096]{1,0:T(8,128)(2,1)}, u32[]{:S(2)}, u32[]{:S(2)}) collective-permute-start(bf16[128,4096]{1,0:T(8,128)(2,1)S(1)} %fusion.132), channel_id=1, source_target_pairs={{0,8},{8,16},{16,24},{24,32},{32,40},{40,48},{48,56},{56,64},{64,7... | collective-permute-start | bytes 3145736 | tf_op jit(solution)/shard_map/ppermute | solution.py:13
  16.7 4.0 copy-start.8
  17.7 16.7 %collective-permute-start.1 = (bf16[128,4096]{1,0:T(8,128)(2,1)}, bf16[128,4096]{1,0:T(8,128)(2,1)}, u32[]{:S(2)}, u32[]{:S(2)}) collective-permute-start(bf16[128,4096]{1,0:T(8,128)(2,1)} %broadcast_select_fusion), channel_id=1, source_target_pairs={{8,0},{16,8},{24,16},{32,24},{40,32},{48,40},{56,48},{64,56},{72,6... | collective-permute-start | bytes 3145736 | tf_op jit(solution)/shard_map/ppermute | solution.py:13
  64.1 6.7 copy-start
  104.1 15.4 %copy-start.2 = (f32[128,4096]{1,0:T(8,128)S(1)}, f32[128,4096]{1,0:T(8,128)}, u32[]{:S(2)}) copy-start(f32[128,4096]{1,0:T(8,128)} %get-tuple-element.668) | copy-start | bytes 6291460 | tf_op jit(solution)/shard_map/while
  129.7 1.3 copy-start.3
  131.2 6.7 copy-start
  171.3 15.7 %copy-start.2 = (f32[128,4096]{1,0:T(8,128)S(1)}, f32[128,4096]{1,0:T(8,128)}, u32[]{:S(2)}) copy-start(f32[128,4096]{1,0:T(8,128)} %get-tuple-element.668) | copy-start | bytes 6291460 | tf_op jit(solution)/shard_map/while
  197.2 1.3 copy-start.3
  198.7 6.7 copy-start
  238.9 15.9 %copy-start.2 = (f32[128,4096]{1,0:T(8,128)S(1)}, f32[128,4096]{1,0:T(8,128)}, u32[]{:S(2)}) copy-start(f32[128,4096]{1,0:T(8,128)} %get-tuple-element.668) | copy-start | bytes 6291460 | tf_op jit(solution)/shard_map/while
  265.0 1.3 copy-start.3
  266.5 6.7 copy-start
  306.4 16.1 %copy-start.2 = (f32[128,4096]{1,0:T(8,128)S(1)}, f32[128,4096]{1,0:T(8,128)}, u32[]{:S(2)}) copy-start(f32[128,4096]{1,0:T(8,128)} %get-tuple-element.668) | copy-start | bytes 6291460 | tf_op jit(solution)/shard_map/while
  334.1 6.7 copy-start
  374.2 15.8 %copy-start.2 = (f32[128,4096]{1,0:T(8,128)S(1)}, f32[128,4096]{1,0:T(8,128)}, u32[]{:S(2)}) copy-start(f32[128,4096]{1,0:T(8,128)} %get-tuple-element.668) | copy-start | bytes 6291460 | tf_op jit(solution)/shard_map/while
  400.1 1.3 copy-start.3
  401.6 6.7 copy-start
  441.6 15.6 %copy-start.2 = (f32[128,4096]{1,0:T(8,128)S(1)}, f32[128,4096]{1,0:T(8,128)}, u32[]{:S(2)}) copy-start(f32[128,4096]{1,0:T(8,128)} %get-tuple-element.668) | copy-start | bytes 6291460 | tf_op jit(solution)/shard_map/while
  467.4 1.3 copy-start.3
  468.9 6.7 copy-start
  508.9 16.1 %copy-start.2 = (f32[128,4096]{1,0:T(8,128)S(1)}, f32[128,4096]{1,0:T(8,128)}, u32[]{:S(2)}) copy-start(f32[128,4096]{1,0:T(8,128)} %get-tuple-element.668) | copy-start | bytes 6291460 | tf_op jit(solution)/shard_map/while
  536.6 6.7 copy-start
  576.9 16.1 %copy-start.2 = (f32[128,4096]{1,0:T(8,128)S(1)}, f32[128,4096]{1,0:T(8,128)}, u32[]{:S(2)}) copy-start(f32[128,4096]{1,0:T(8,128)} %get-tuple-element.668) | copy-start | bytes 6291460 | tf_op jit(solution)/shard_map/while
  604.4 3.3 copy-start.4
  607.6 1.6 copy-start.1
  607.6 167.7 %all-reduce.2.cloned.1.call-start = ((), (), s32[]{:S(2)}) async-start(), calls=%async_computation.3 | async-start | bytes 1048576 | tf_op jit(solution)/shard_map/psum | solution.py:86
  (3 other events, 4.0 us)
Sparse Core Ops, SparseCore 0:
  9.8 52.5 all-gather.1
  607.7 51.7 reduce-scatter.1
  663.0 112.2 all-reduce.1
where the time goes:
time: 787 us; the launch traced here: 784 us
  other arithmetic  323 us (41%)
  local copies, waits for them, and re-layouts  240 us (30%)
  waiting for transfers between devices  198 us (25%)
  between operations  14.5 us (2%)
    dynamic_update_slice x128, local copies, waits for them, and re-layouts, tap_block(): lax.dynamic_update_slice_in_dim(filt_grad, tap_term[None, :], tap_index, 0)  205 us
    add x8, other arithmetic, tap_block(): grad_back = grad_back + jnp.where(reaching, ahead_rows * weight_row, 0.0)  127 us
    psum x1, waiting for transfers between devices, shards(): summed_all = lax.psum(filt_grad, 'ctx')  113 us
    reduce_sum x16, other arithmetic, tap_block(): tap_term = jnp.sum(jnp.where(inside, grad_wide * earlier, 0.0), axis=0)  95.8 us
    add x8, other arithmetic, tap_block(): conv_out = conv_out + jnp.where(inside, earlier * weight_row, 0.0)  80.8 us
    reduce_scatter x1, waiting for transfers between devices, shards(): lax.psum_scatter(summed_all, 'fsdp', scatter_dimension=0, tiled=True)  47.3 us
    all_gather x1, waiting for transfers between devices, shards(): weights = lax.all_gather(filters, 'fsdp', axis=0, tiled=True)  25.2 us
    dynamic_slice x8, local copies, waits for them, and re-layouts, tap_block(): weight_row = lax.dynamic_slice_in_dim(weights, tap_index, 1, 0)  19.3 us
  transfers between devices with their start and end apart: 5, of which 5 were waited for; matrix products, arithmetic and copies ran while one was open for 2% of the time, Pallas kernels for 0%

commit v1 on v0

--- a/solution.py
+++ b/solution.py
@@ -83,7 +83,11 @@
     grad_value = (grad_back * key_local.astype(jnp.float32)).astype(jnp.bfloat16)
     norm_scale = 1.0 / math.sqrt(lax.axis_size("fsdp") * lax.axis_size("ctx") * length)
     filt_grad = filt_grad * norm_scale
-    summed_all = lax.psum(filt_grad, "ctx")
+    summed_all = filt_grad
+    for hop in (1, 2, 4, 8, 16):
+        summed_all = summed_all + lax.ppermute(
+            summed_all, "ctx", [(dev, dev ^ hop) for dev in range(32)]
+        )
     share_out = lax.psum_scatter(summed_all, "fsdp", scatter_dimension=0, tiled=True)
     return (grad_query[None], grad_key[None], grad_value[None], share_out)
 

time: 787 us -> 864 us (1.098)
  waiting for transfers between devices: 198 us -> 266 us
  starting transfers between devices: 7.53 us -> 18.1 us
    ppermute x0 -> x5, waiting for transfers between devices: none -> 183 us  [shards(): lax.ppermute(summed_all, 'ctx', [(dev, dev ^ hop) for dev in range(32)])]
    psum x1 -> x0, waiting for transfers between devices: 113 us -> none  [shards(): summed_all = lax.psum(filt_grad, 'ctx')]
    ppermute x0 -> x5, starting transfers between devices: none -> 10.6 us  [shards(): lax.ppermute(summed_all, 'ctx', [(dev, dev ^ hop) for dev in range(32)])]
  transfers between devices with their start and end apart: 5 -> 9, of which waited for: 5 -> 9; matrix products, arithmetic and copies ran while one was open for 2% -> 2% of each run, Pallas kernels for 0% -> 0%
where the time goes in v1:
time: 864 us; the launch traced here: 861 us
  other arithmetic  323 us (37%)
  waiting for transfers between devices  266 us (31%)
  local copies, waits for them, and re-layouts  238 us (28%)
  starting transfers between devices  18.1 us (2%)
  between operations  14.9 us (2%)
    dynamic_update_slice x128, local copies, waits for them, and re-layouts, tap_block(): lax.dynamic_update_slice_in_dim(filt_grad, tap_term[None, :], tap_index, 0)  205 us
    ppermute x5, waiting for transfers between devices, shards(): lax.ppermute(summed_all, 'ctx', [(dev, dev ^ hop) for dev in range(32)])  183 us
    add x8, other arithmetic, tap_block(): grad_back = grad_back + jnp.where(reaching, ahead_rows * weight_row, 0.0)  127 us
    reduce_sum x16, other arithmetic, tap_block(): tap_term = jnp.sum(jnp.where(inside, grad_wide * earlier, 0.0), axis=0)  95.8 us
    add x8, other arithmetic, tap_block(): conv_out = conv_out + jnp.where(inside, earlier * weight_row, 0.0)  80.8 us
    reduce_scatter x1, waiting for transfers between devices, shards(): lax.psum_scatter(summed_all, 'fsdp', scatter_dimension=0, tiled=True)  45.1 us
    all_gather x1, waiting for transfers between devices, shards(): weights = lax.all_gather(filters, 'fsdp', axis=0, tiled=True)  25.2 us
    dynamic_slice x8, local copies, waits for them, and re-layouts, tap_block(): weight_row = lax.dynamic_slice_in_dim(weights, tap_index, 1, 0)  19.3 us
  transfers between devices with their start and end apart: 9, of which 9 were waited for; matrix products, arithmetic and copies ran while one was open for 2% of the time, Pallas kernels for 0%

profile of v1, /device:TPU:1, one launch (start us, length us, event | category | flops | bytes accessed | tf_op | source)
XLA Modules:
  0.0 860.7 jit_solution(12973702303083749387)
XLA Ops:
  28.0 6.5 collective-permute-done.1
  37.2 25.2 %all-gather.2.cloned.1.call-done = f32[128,4096]{1,0:T(8,128)} async-done(((f32[32,4096]{1,0:T(8,128)}), f32[128,4096]{1,0:T(8,128)}) %all-gather.2.cloned.1.call-update) | async-done | bytes 2097168 | tf_op jit(solution)/shard_map/all_gather | solution.py:22
  63.9 540.4 %while.18 = (s32[]{:T(128)}, f32[128,4096]{1,0:T(8,128)}, f32[128,4096]{1,0:T(8,128)}, f32[128,4096]{1,0:T(8,128)}, s32[128]{0:T(128)S(1)}, /*index=5*/bf16[256,...) while((s32[]{:T(128)}, f32[128,4096]{1,0:T(8,128)}, ...), condition=%wide.region_19.20_spmd.clone, body=%wide.region_2.19_spmd.clone.sunk | while | flops 101652864 | bytes 89937200 | solution.py:78
  64.1 6.7 fusion.151
  104.1 15.4 %fusion.149 = f32[128,4096]{1,0:T(8,128)} fusion(f32[128,4096]{1,0:T(8,128)} %get-tuple-element.669, bf16[256,4096]{1,0:T(8,128)(2,1)} %get-tuple-element.736, s32[]{:T(128)S(6)} %select_n.1126, s32[]{:T(128)S(6)} %select_n.1127, s32[]{:T(128)S(6)} %select_n.1128, s32[]{:T(128)S(6)} %select_n.1129, s32[]{:T(128)S(6)} %select_n.1130, ...), kind=kLoop, calls=%fused_computation.112.clone.1 | loop fusion | flops 34078720 | bytes 21235776 | tf_op jit(solution)/shard_map/while/body/add | solution.py:70
  119.5 10.1 %fusion.147 = f32[128,4096]{1,0:T(8,128)S(1)} fusion(f32[128,4096]{1,0:T(8,128)S(1)} %copy-done.2, f32[4096]{0:T(1024)S(1)} %bitcast.124, f32[4096]{0:T(1024)S(1)} %bitcast.126, f32[4096]{0:T(1024)S(1)} %bitcast.128, f32[4096]{0:T(1024)S(1)} %bitcast.130, f32[4096]{0:T(1024)S(1)} %bitcast.132, f32[4096]{0:T(1024)S(1)} %bitcast.134, ...), kind=kLoop, calls=%fused_computation.49.clone.1 | loop fusion | flops 34078720 | bytes 21235776 | tf_op jit(solution)/shard_map/while/body/add | solution.py:61
  131.2 6.7 fusion.151
  171.3 15.7 %fusion.149 = f32[128,4096]{1,0:T(8,128)} fusion(f32[128,4096]{1,0:T(8,128)} %get-tuple-element.669, bf16[256,4096]{1,0:T(8,128)(2,1)} %get-tuple-element.736, s32[]{:T(128)S(6)} %select_n.1126, s32[]{:T(128)S(6)} %select_n.1127, s32[]{:T(128)S(6)} %select_n.1128, s32[]{:T(128)S(6)} %select_n.1129, s32[]{:T(128)S(6)} %select_n.1130, ...), kind=kLoop, calls=%fused_computation.112.clone.1 | loop fusion | flops 34078720 | bytes 21235776 | tf_op jit(solution)/shard_map/while/body/add | solution.py:70
  187.1 10.1 %fusion.147 = f32[128,4096]{1,0:T(8,128)S(1)} fusion(f32[128,4096]{1,0:T(8,128)S(1)} %copy-done.2, f32[4096]{0:T(1024)S(1)} %bitcast.124, f32[4096]{0:T(1024)S(1)} %bitcast.126, f32[4096]{0:T(1024)S(1)} %bitcast.128, f32[4096]{0:T(1024)S(1)} %bitcast.130, f32[4096]{0:T(1024)S(1)} %bitcast.132, f32[4096]{0:T(1024)S(1)} %bitcast.134, ...), kind=kLoop, calls=%fused_computation.49.clone.1 | loop fusion | flops 34078720 | bytes 21235776 | tf_op jit(solution)/shard_map/while/body/add | solution.py:61
  198.7 6.7 fusion.151
  238.9 15.9 %fusion.149 = f32[128,4096]{1,0:T(8,128)} fusion(f32[128,4096]{1,0:T(8,128)} %get-tuple-element.669, bf16[256,4096]{1,0:T(8,128)(2,1)} %get-tuple-element.736, s32[]{:T(128)S(6)} %select_n.1126, s32[]{:T(128)S(6)} %select_n.1127, s32[]{:T(128)S(6)} %select_n.1128, s32[]{:T(128)S(6)} %select_n.1129, s32[]{:T(128)S(6)} %select_n.1130, ...), kind=kLoop, calls=%fused_computation.112.clone.1 | loop fusion | flops 34078720 | bytes 21235776 | tf_op jit(solution)/shard_map/while/body/add | solution.py:70
  254.9 10.1 %fusion.147 = f32[128,4096]{1,0:T(8,128)S(1)} fusion(f32[128,4096]{1,0:T(8,128)S(1)} %copy-done.2, f32[4096]{0:T(1024)S(1)} %bitcast.124, f32[4096]{0:T(1024)S(1)} %bitcast.126, f32[4096]{0:T(1024)S(1)} %bitcast.128, f32[4096]{0:T(1024)S(1)} %bitcast.130, f32[4096]{0:T(1024)S(1)} %bitcast.132, f32[4096]{0:T(1024)S(1)} %bitcast.134, ...), kind=kLoop, calls=%fused_computation.49.clone.1 | loop fusion | flops 34078720 | bytes 21235776 | tf_op jit(solution)/shard_map/while/body/add | solution.py:61
  266.5 6.7 fusion.151
  306.4 16.0 %fusion.149 = f32[128,4096]{1,0:T(8,128)} fusion(f32[128,4096]{1,0:T(8,128)} %get-tuple-element.669, bf16[256,4096]{1,0:T(8,128)(2,1)} %get-tuple-element.736, s32[]{:T(128)S(6)} %select_n.1126, s32[]{:T(128)S(6)} %select_n.1127, s32[]{:T(128)S(6)} %select_n.1128, s32[]{:T(128)S(6)} %select_n.1129, s32[]{:T(128)S(6)} %select_n.1130, ...), kind=kLoop, calls=%fused_computation.112.clone.1 | loop fusion | flops 34078720 | bytes 21235776 | tf_op jit(solution)/shard_map/while/body/add | solution.py:70
  322.5 10.1 %fusion.147 = f32[128,4096]{1,0:T(8,128)S(1)} fusion(f32[128,4096]{1,0:T(8,128)S(1)} %copy-done.2, f32[4096]{0:T(1024)S(1)} %bitcast.124, f32[4096]{0:T(1024)S(1)} %bitcast.126, f32[4096]{0:T(1024)S(1)} %bitcast.128, f32[4096]{0:T(1024)S(1)} %bitcast.130, f32[4096]{0:T(1024)S(1)} %bitcast.132, f32[4096]{0:T(1024)S(1)} %bitcast.134, ...), kind=kLoop, calls=%fused_computation.49.clone.1 | loop fusion | flops 34078720 | bytes 21235776 | tf_op jit(solution)/shard_map/while/body/add | solution.py:61
  334.1 6.7 fusion.151
  374.2 15.8 %fusion.149 = f32[128,4096]{1,0:T(8,128)} fusion(f32[128,4096]{1,0:T(8,128)} %get-tuple-element.669, bf16[256,4096]{1,0:T(8,128)(2,1)} %get-tuple-element.736, s32[]{:T(128)S(6)} %select_n.1126, s32[]{:T(128)S(6)} %select_n.1127, s32[]{:T(128)S(6)} %select_n.1128, s32[]{:T(128)S(6)} %select_n.1129, s32[]{:T(128)S(6)} %select_n.1130, ...), kind=kLoop, calls=%fused_computation.112.clone.1 | loop fusion | flops 34078720 | bytes 21235776 | tf_op jit(solution)/shard_map/while/body/add | solution.py:70
  390.0 10.1 %fusion.147 = f32[128,4096]{1,0:T(8,128)S(1)} fusion(f32[128,4096]{1,0:T(8,128)S(1)} %copy-done.2, f32[4096]{0:T(1024)S(1)} %bitcast.124, f32[4096]{0:T(1024)S(1)} %bitcast.126, f32[4096]{0:T(1024)S(1)} %bitcast.128, f32[4096]{0:T(1024)S(1)} %bitcast.130, f32[4096]{0:T(1024)S(1)} %bitcast.132, f32[4096]{0:T(1024)S(1)} %bitcast.134, ...), kind=kLoop, calls=%fused_computation.49.clone.1 | loop fusion | flops 34078720 | bytes 21235776 | tf_op jit(solution)/shard_map/while/body/add | solution.py:61
  401.6 6.7 fusion.151
  441.6 15.6 %fusion.149 = f32[128,4096]{1,0:T(8,128)} fusion(f32[128,4096]{1,0:T(8,128)} %get-tuple-element.669, bf16[256,4096]{1,0:T(8,128)(2,1)} %get-tuple-element.736, s32[]{:T(128)S(6)} %select_n.1126, s32[]{:T(128)S(6)} %select_n.1127, s32[]{:T(128)S(6)} %select_n.1128, s32[]{:T(128)S(6)} %select_n.1129, s32[]{:T(128)S(6)} %select_n.1130, ...), kind=kLoop, calls=%fused_computation.112.clone.1 | loop fusion | flops 34078720 | bytes 21235776 | tf_op jit(solution)/shard_map/while/body/add | solution.py:70
  457.3 10.1 %fusion.147 = f32[128,4096]{1,0:T(8,128)S(1)} fusion(f32[128,4096]{1,0:T(8,128)S(1)} %copy-done.2, f32[4096]{0:T(1024)S(1)} %bitcast.124, f32[4096]{0:T(1024)S(1)} %bitcast.126, f32[4096]{0:T(1024)S(1)} %bitcast.128, f32[4096]{0:T(1024)S(1)} %bitcast.130, f32[4096]{0:T(1024)S(1)} %bitcast.132, f32[4096]{0:T(1024)S(1)} %bitcast.134, ...), kind=kLoop, calls=%fused_computation.49.clone.1 | loop fusion | flops 34078720 | bytes 21235776 | tf_op jit(solution)/shard_map/while/body/add | solution.py:61
  468.9 6.7 fusion.151
  508.9 16.1 %fusion.149 = f32[128,4096]{1,0:T(8,128)} fusion(f32[128,4096]{1,0:T(8,128)} %get-tuple-element.669, bf16[256,4096]{1,0:T(8,128)(2,1)} %get-tuple-element.736, s32[]{:T(128)S(6)} %select_n.1126, s32[]{:T(128)S(6)} %select_n.1127, s32[]{:T(128)S(6)} %select_n.1128, s32[]{:T(128)S(6)} %select_n.1129, s32[]{:T(128)S(6)} %select_n.1130, ...), kind=kLoop, calls=%fused_computation.112.clone.1 | loop fusion | flops 34078720 | bytes 21235776 | tf_op jit(solution)/shard_map/while/body/add | solution.py:70
  525.0 10.1 %fusion.147 = f32[128,4096]{1,0:T(8,128)S(1)} fusion(f32[128,4096]{1,0:T(8,128)S(1)} %copy-done.2, f32[4096]{0:T(1024)S(1)} %bitcast.124, f32[4096]{0:T(1024)S(1)} %bitcast.126, f32[4096]{0:T(1024)S(1)} %bitcast.128, f32[4096]{0:T(1024)S(1)} %bitcast.130, f32[4096]{0:T(1024)S(1)} %bitcast.132, f32[4096]{0:T(1024)S(1)} %bitcast.134, ...), kind=kLoop, calls=%fused_computation.49.clone.1 | loop fusion | flops 34078720 | bytes 21235776 | tf_op jit(solution)/shard_map/while/body/add | solution.py:61
  536.6 6.7 fusion.151
  576.9 16.1 %fusion.149 = f32[128,4096]{1,0:T(8,128)} fusion(f32[128,4096]{1,0:T(8,128)} %get-tuple-element.669, bf16[256,4096]{1,0:T(8,128)(2,1)} %get-tuple-element.736, s32[]{:T(128)S(6)} %select_n.1126, s32[]{:T(128)S(6)} %select_n.1127, s32[]{:T(128)S(6)} %select_n.1128, s32[]{:T(128)S(6)} %select_n.1129, s32[]{:T(128)S(6)} %select_n.1130, ...), kind=kLoop, calls=%fused_computation.112.clone.1 | loop fusion | flops 34078720 | bytes 21235776 | tf_op jit(solution)/shard_map/while/body/add | solution.py:70
  592.9 10.1 %fusion.147 = f32[128,4096]{1,0:T(8,128)S(1)} fusion(f32[128,4096]{1,0:T(8,128)S(1)} %copy-done.2, f32[4096]{0:T(1024)S(1)} %bitcast.124, f32[4096]{0:T(1024)S(1)} %bitcast.126, f32[4096]{0:T(1024)S(1)} %bitcast.128, f32[4096]{0:T(1024)S(1)} %bitcast.130, f32[4096]{0:T(1024)S(1)} %bitcast.132, f32[4096]{0:T(1024)S(1)} %bitcast.134, ...), kind=kLoop, calls=%fused_computation.49.clone.1 | loop fusion | flops 34078720 | bytes 21235776 | tf_op jit(solution)/shard_map/while/body/add | solution.py:61
  615.5 45.7 %collective-permute-done.3 = f32[128,4096]{1,0:T(8,128)S(1)} collective-permute-done((f32[128,4096]{1,0:T(8,128)S(1)}, f32[128,4096]{1,0:T(8,128)S(1)}, u32[]{:S(2)}, u32[]{:S(2)}) %collective-permute-start.3) | collective-permute-done | bytes 2097184 | tf_op jit(solution)/shard_map/ppermute | solution.py:88
  664.0 45.2 %collective-permute-done.4 = f32[128,4096]{1,0:T(8,128)S(1)} collective-permute-done((f32[128,4096]{1,0:T(8,128)S(1)}, f32[128,4096]{1,0:T(8,128)S(1)}, u32[]{:S(2)}, u32[]{:S(2)}) %collective-permute-start.4) | collective-permute-done | bytes 2097184 | tf_op jit(solution)/shard_map/ppermute | solution.py:88
  710.3 44.6 %collective-permute-done.5 = f32[128,4096]{1,0:T(8,128)S(1)} collective-permute-done((f32[128,4096]{1,0:T(8,128)S(1)}, f32[128,4096]{1,0:T(8,128)S(1)}, u32[]{:S(2)}, u32[]{:S(2)}) %collective-permute-start.5) | collective-permute-done | bytes 2097184 | tf_op jit(solution)/shard_map/ppermute | solution.py:88
  757.2 44.0 %collective-permute-done.6 = f32[128,4096]{1,0:T(8,128)S(1)} collective-permute-done((f32[128,4096]{1,0:T(8,128)S(1)}, f32[128,4096]{1,0:T(8,128)S(1)}, u32[]{:S(2)}, u32[]{:S(2)}) %collective-permute-start.6) | collective-permute-done | bytes 2097184 | tf_op jit(solution)/shard_map/ppermute | solution.py:88
  808.8 45.1 %reduce-scatter.2.cloned.1.call-done = f32[32,4096]{1,0:T(8,128)} async-done(((f32[128,4096]{1,0:T(8,128)}), f32[32,4096]{1,0:T(8,128)}) %reduce-scatter.2.cloned.1.call-update) | async-done | bytes 524304 | tf_op jit(solution)/shard_map/reduce_scatter | solution.py:91
  (259 shorter events, 328.1 us)
Async XLA Ops:
  7.2 7.9 copy-start.5
  7.2 55.2 %all-gather.2.cloned.1.call-start = ((), (), s32[]{:S(2)}) async-start(), calls=%async_computation.1 | async-start | bytes 2621440 | tf_op jit(solution)/shard_map/all_gather | solution.py:22
  7.9 846.0 %reduce-scatter.2.cloned.1.call-start = ((), (), s32[]{:S(2)}) async-start(), calls=%async_computation.2 | async-start | bytes 2621440 | tf_op jit(solution)/shard_map/reduce_scatter | solution.py:91
  8.0 7.1 copy-start.10
  9.8 6.8 copy-start.9
  9.9 16.2 %collective-permute-start = (bf16[128,4096]{1,0:T(8,128)(2,1)S(1)}, bf16[128,4096]{1,0:T(8,128)(2,1)}, u32[]{:S(2)}, u32[]{:S(2)}) collective-permute-start(bf16[128,4096]{1,0:T(8,128)(2,1)S(1)} %fusion.132), channel_id=1, source_target_pairs={{0,8},{8,16},{16,24},{24,32},{32,40},{40,48},{48,56},{56,64},{64,7... | collective-permute-start | bytes 3145736 | tf_op jit(solution)/shard_map/ppermute | solution.py:13
  16.7 4.0 copy-start.11
  17.7 16.7 %collective-permute-start.1 = (bf16[128,4096]{1,0:T(8,128)(2,1)}, bf16[128,4096]{1,0:T(8,128)(2,1)}, u32[]{:S(2)}, u32[]{:S(2)}) collective-permute-start(bf16[128,4096]{1,0:T(8,128)(2,1)} %broadcast_select_fusion), channel_id=1, source_target_pairs={{8,0},{16,8},{24,16},{32,24},{40,32},{48,40},{56,48},{64,56},{72,6... | collective-permute-start | bytes 3145736 | tf_op jit(solution)/shard_map/ppermute | solution.py:13
  64.1 6.7 copy-start
  104.1 15.4 %copy-start.2 = (f32[128,4096]{1,0:T(8,128)S(1)}, f32[128,4096]{1,0:T(8,128)}, u32[]{:S(2)}) copy-start(f32[128,4096]{1,0:T(8,128)} %get-tuple-element.668) | copy-start | bytes 6291460 | tf_op jit(solution)/shard_map/while
  131.2 6.7 copy-start
  171.3 15.7 %copy-start.2 = (f32[128,4096]{1,0:T(8,128)S(1)}, f32[128,4096]{1,0:T(8,128)}, u32[]{:S(2)}) copy-start(f32[128,4096]{1,0:T(8,128)} %get-tuple-element.668) | copy-start | bytes 6291460 | tf_op jit(solution)/shard_map/while
  198.7 6.7 copy-start
  238.9 15.9 %copy-start.2 = (f32[128,4096]{1,0:T(8,128)S(1)}, f32[128,4096]{1,0:T(8,128)}, u32[]{:S(2)}) copy-start(f32[128,4096]{1,0:T(8,128)} %get-tuple-element.668) | copy-start | bytes 6291460 | tf_op jit(solution)/shard_map/while
  266.5 6.7 copy-start
  306.4 16.1 %copy-start.2 = (f32[128,4096]{1,0:T(8,128)S(1)}, f32[128,4096]{1,0:T(8,128)}, u32[]{:S(2)}) copy-start(f32[128,4096]{1,0:T(8,128)} %get-tuple-element.668) | copy-start | bytes 6291460 | tf_op jit(solution)/shard_map/while
  334.1 6.7 copy-start
  374.2 15.8 %copy-start.2 = (f32[128,4096]{1,0:T(8,128)S(1)}, f32[128,4096]{1,0:T(8,128)}, u32[]{:S(2)}) copy-start(f32[128,4096]{1,0:T(8,128)} %get-tuple-element.668) | copy-start | bytes 6291460 | tf_op jit(solution)/shard_map/while
  401.6 6.7 copy-start
  441.6 15.6 %copy-start.2 = (f32[128,4096]{1,0:T(8,128)S(1)}, f32[128,4096]{1,0:T(8,128)}, u32[]{:S(2)}) copy-start(f32[128,4096]{1,0:T(8,128)} %get-tuple-element.668) | copy-start | bytes 6291460 | tf_op jit(solution)/shard_map/while
  468.9 6.7 copy-start
  508.9 16.1 %copy-start.2 = (f32[128,4096]{1,0:T(8,128)S(1)}, f32[128,4096]{1,0:T(8,128)}, u32[]{:S(2)}) copy-start(f32[128,4096]{1,0:T(8,128)} %get-tuple-element.668) | copy-start | bytes 6291460 | tf_op jit(solution)/shard_map/while
  536.6 6.7 copy-start
  576.9 16.1 %copy-start.2 = (f32[128,4096]{1,0:T(8,128)S(1)}, f32[128,4096]{1,0:T(8,128)}, u32[]{:S(2)}) copy-start(f32[128,4096]{1,0:T(8,128)} %get-tuple-element.668) | copy-start | bytes 6291460 | tf_op jit(solution)/shard_map/while
  604.4 6.5 copy-start.4
  606.3 4.6 collective-permute-start.2
  611.2 50.0 %collective-permute-start.3 = (f32[128,4096]{1,0:T(8,128)S(1)}, f32[128,4096]{1,0:T(8,128)S(1)}, u32[]{:S(2)}, u32[]{:S(2)}) collective-permute-start(f32[128,4096]{1,0:T(8,128)S(1)} %fusion.137), channel_id=1, source_target_pairs={{0,16},{8,24},{16,0},{24,8},{32,48},{40,56},{48,32},{56,40},{64,80... | collective-permute-start | bytes 6291464 | tf_op jit(solution)/shard_map/ppermute | solution.py:88
  661.4 47.9 %collective-permute-start.4 = (f32[128,4096]{1,0:T(8,128)S(1)}, f32[128,4096]{1,0:T(8,128)S(1)}, u32[]{:S(2)}, u32[]{:S(2)}) collective-permute-start(f32[128,4096]{1,0:T(8,128)S(1)} %add.854), channel_id=1, source_target_pairs={{0,32},{8,40},{16,48},{24,56},{32,0},{40,8},{48,16},{56,24},{64,96... | collective-permute-start | bytes 6291464 | tf_op jit(solution)/shard_map/ppermute | solution.py:88
  709.5 45.4 %collective-permute-start.5 = (f32[128,4096]{1,0:T(8,128)S(1)}, f32[128,4096]{1,0:T(8,128)S(1)}, u32[]{:S(2)}, u32[]{:S(2)}) collective-permute-start(f32[128,4096]{1,0:T(8,128)S(1)} %add.855), channel_id=1, source_target_pairs={{0,64},{8,72},{16,80},{24,88},{32,96},{40,104},{48,112},{56,120},{... | collective-permute-start | bytes 6291464 | tf_op jit(solution)/shard_map/ppermute | solution.py:88
  755.2 46.0 %collective-permute-start.6 = (f32[128,4096]{1,0:T(8,128)S(1)}, f32[128,4096]{1,0:T(8,128)S(1)}, u32[]{:S(2)}, u32[]{:S(2)}) collective-permute-start(f32[128,4096]{1,0:T(8,128)S(1)} %add.856), channel_id=1, source_target_pairs={{0,128},{8,136},{16,144},{24,152},{32,160},{40,168},{48,176},{56,1... | collective-permute-start | bytes 6291464 | tf_op jit(solution)/shard_map/ppermute | solution.py:88
  804.0 2.9 copy-start.7
  804.0 2.9 copy-start.8
  (10 other events, 14.9 us)
Sparse Core Ops, SparseCore 0:
  9.8 52.5 all-gather.1
  803.0 50.8 reduce-scatter.1
